TPU v7x, 256 devices: a whole 4x4x8 slice. The times are simulated.
256 devices in a mesh: row: 16 (over y_lo, z), col: 16 (over y_hi, x, core).
Axes of the slice: x: 4, y: 4 (y_hi: 2, y_lo: 2; y = y_hi * 2 + y_lo), z: 8, core: 2. Of those that a mesh axis runs over, the one named last changes fastest.
Arguments:
- early_coords: bfloat16 [64, 32768], P(None, ('row', 'col')), may hold values from -13 to 13
- late_coords: bfloat16 [64, 131072], P(None, ('row', 'col')), may hold values from -13 to 13
- late_log_scale: bfloat16 [131072], P(('row', 'col')), may hold values from -2 to 115
- fate_labels: int32 [32768], P(('row', 'col')), may hold values from 0 to 255, as said below
- loadings: float32 [64, 2000], replicated, may hold values from -0.75 to 0.75
Outputs:
- projected: float32 [64, 32768], P(None, ('row', 'col'))
- fate_corr: float32 [2000, 256], replicated
Inputs may be any that keep to these rules, and one draw needn't show every extreme that they name: `fate_labels`: every one of the 256 fate classes labels at least one early cell.
All inputs are finite; a program needn't handle non-finite values.
Results may differ from a plain program's by a relative error of at most 0.0003.
Values may be sent and summed in bfloat16 or wider, within the bound.
No kernel may reach another device: no remote copies, remote signals or barrier semaphores. Data moves between devices by JAX's collectives and lax.ppermute only.
A program may use at most 64 MiB of HBM per device.

v0:
```python
import functools
import math

import jax
import jax.numpy as jnp
from jax import lax
from jax.experimental import pallas as pl
from jax.experimental.pallas import tpu as pltpu
from jax.sharding import Mesh
from jax.sharding import PartitionSpec as P


f32 = jnp.float32
bf16 = jnp.bfloat16

DIM = 64
FATES = 256
EPSILON = 1e-06
SHARP = 8.0 / DIM
LOG2E = math.log2(math.e)
LOWEST = -1e30

AXES = ("yl", "z", "yh", "x", "core")
SIZES = (2, 8, 2, 4, 2)
PLANE = ("yl", "yh", "x", "core")

LINE_ORDER = (2, 1, 3, 0)


def split3(v):
    high = v.astype(bf16).astype(f32)
    rest = v - high
    mid = rest.astype(bf16).astype(f32)
    return high, mid, rest - mid


def put_rows(base, row, first, value):
    for k, piece in enumerate(split3(value)):
        base = jnp.where(row == first + k, piece, base)
    return base


def pack_kernel(late_ref, log_ref, all_ref):
    cells = late_ref.shape[1]
    blocks = [late_ref[:, 128 * k : 128 * (k + 1)] for k in range(cells // 128)]
    logs = [log_ref[:, 128 * k : 128 * (k + 1)].astype(f32) for k in range(cells // 128)]
    tail = jnp.concatenate(logs + [jnp.zeros((8 - cells // 128, 128), f32)], 0).astype(bf16)
    one = jnp.concatenate(blocks + [tail], 0)
    for k in range(all_ref.shape[0]):
        all_ref[k] = one


def pack(late, logs, copies):
    rows = DIM * late.shape[1] // 128 + 8
    return pl.pallas_call(
        pack_kernel,
        out_shape=jax.ShapeDtypeStruct((copies, rows, 128), bf16),
        in_specs=[pl.BlockSpec(memory_space=pltpu.VMEM)] * 2,
        out_specs=pl.BlockSpec(memory_space=pltpu.VMEM),
        compiler_params=pltpu.CompilerParams(vmem_limit_bytes=8 * 2**20),
        name="pack",
    )(late, logs[None])


def ready_kernel(late_ref, ya_ref, yw_ref):
    chunk = (late_ref.shape[1] - 8) * 2
    groups = chunk // 128
    row = lax.broadcasted_iota(jnp.int32, (DIM, chunk), 0)
    lane = lax.broadcasted_iota(jnp.int32, (chunk, 128), 1)
    blank = jnp.where((row >= 3) & (row < 6), 1.0, jnp.zeros((DIM, chunk), f32))
    ones = jnp.where(lax.broadcasted_iota(jnp.int32, (16, chunk), 0) == 0, 1.0, 0.0).astype(bf16)
    for b in range(late_ref.shape[0]):
        yb = jnp.concatenate([late_ref[b, DIM * k : DIM * (k + 1), :] for k in range(groups)], 1)
        tail = late_ref[b, DIM * groups : DIM * groups + 8, :].astype(f32)
        logs = jnp.concatenate([tail[k : k + 1] for k in range(groups)], 1)
        y = yb.astype(f32)
        bias = (logs - jnp.sum(y * y, 0, keepdims=True) * SHARP) * LOG2E
        t = jnp.concatenate([y, put_rows(blank, row, 0, bias)], 0).T
        twice = jnp.where(lane < DIM, t, pltpu.roll(t, DIM, 1))
        ya_ref[b * chunk : (b + 1) * chunk, :] = jnp.concatenate([t, twice], 1).astype(bf16)
        yw_ref[:, b * chunk : (b + 1) * chunk] = jnp.concatenate([yb, ones], 0)


def ready(late):
    total = late.shape[0] * (late.shape[1] - 8) * 2
    return pl.pallas_call(
        ready_kernel,
        out_shape=(
            jax.ShapeDtypeStruct((total, 256), bf16),
            jax.ShapeDtypeStruct((80, total), bf16),
        ),
        in_specs=[pl.BlockSpec(memory_space=pltpu.VMEM)],
        out_specs=(pl.BlockSpec(memory_space=pltpu.VMEM),) * 2,
        compiler_params=pltpu.CompilerParams(vmem_limit_bytes=16 * 2**20),
    )(late)


def line_kernel(x_ref, ya0, yw0, ya1, yw1, out_ref, xa, sbuf, mbuf, acc, *, tile, sub):
    wide = 256
    pairs = x_ref.shape[0] // 2
    halves = ((ya0, yw0), (ya1, yw1))
    per_half = ya0.shape[0] // tile
    row = lax.broadcasted_iota(jnp.int32, (DIM, wide), 0)
    blank = jnp.where(row < 3, 1.0, jnp.zeros((DIM, wide), f32))
    for b in range(pairs):
        x = jnp.concatenate([x_ref[2 * b], x_ref[2 * b + 1]], 1).astype(f32)
        norms = jnp.sum(x * x, 0, keepdims=True)
        high, mid, low = split3(x * (2.0 * SHARP * LOG2E))
        extra = put_rows(blank, row, 3, norms * (-SHARP * LOG2E))
        xa[b] = jnp.concatenate([high, extra, mid, low], 0).astype(bf16)

    offsets = range(0, tile, sub)

    def score_part(i, half, offset, top):
        first = pl.multiple_of(i % per_half * tile, tile)
        rows = halves[half][0][pl.ds(first + offset, sub), :]
        s = jnp.dot(rows, xa[i // per_half], preferred_element_type=f32)
        sbuf[half, offset : offset + sub, :] = s
        here = jnp.max(s.reshape(sub // 8, 8, wide), 0)
        return here if top is None else jnp.maximum(top, here)

    def step(i, half, before, last):
        first = pl.multiple_of(i % per_half * tile, tile)
        now = jnp.max(mbuf[half], 0, keepdims=True)
        if half == 0:
            before = jnp.where(i % per_half == 0, LOWEST, before)
        now = jnp.maximum(before, now)
        top = None
        sums = None
        for offset in offsets:
            if not last:
                top = score_part(i + half, 1 - half, offset, top)
            weights = jnp.exp2(sbuf[half, offset : offset + sub, :] - now).astype(bf16)
            columns = halves[half][1][:, pl.ds(first + offset, sub)]
            more = jnp.dot(columns, weights, preferred_element_type=f32)
            sums = more if sums is None else sums + more
        if not last:
            mbuf[1 - half] = top
        total = acc[...] * jnp.exp2(before - now) + sums[:72]
        acc[...] = total
        if half == 1:
            b = i // per_half
            where = lax.broadcasted_iota(jnp.int32, (72, wide), 0)
            packed = jnp.where(where == DIM + 1, now, total)
            out_ref[2 * b] = packed[:, :128]
            out_ref[2 * b + 1] = packed[:, 128:]
        return now

    acc[...] = jnp.zeros_like(acc)
    top = None
    for offset in offsets:
        top = score_part(0, 0, offset, top)
    mbuf[0] = top

    def two_steps(i, before):
        return step(i, 1, step(i, 0, before, False), False)

    rounds = pairs * per_half
    before = lax.fori_loop(0, rounds - 1, two_steps, jnp.full((1, wide), LOWEST, f32))
    step(rounds - 1, 1, step(rounds - 1, 0, before, False), True)


def attend_line(line, own, other, tile=2048, sub=512):
    return pl.pallas_call(
        functools.partial(line_kernel, tile=tile, sub=sub),
        out_shape=jax.ShapeDtypeStruct((line.shape[0], 72, 128), f32),
        in_specs=[pl.BlockSpec(memory_space=pltpu.VMEM)] * 5,
        out_specs=pl.BlockSpec(memory_space=pltpu.VMEM),
        scratch_shapes=[
            pltpu.VMEM((line.shape[0] // 2, 256, 256), bf16),
            pltpu.VMEM((2, tile, 256), f32),
            pltpu.VMEM((2, 8, 256), f32),
            pltpu.VMEM((72, 256), f32),
        ],
        compiler_params=pltpu.CompilerParams(vmem_limit_bytes=24 * 2**20),
    )(line, *own, *other)


def combine_kernel(slot_ref, *refs):
    out_ref = refs[-1]
    parts = refs[:-1]
    row = lax.broadcasted_iota(jnp.int32, (72, 128), 0)
    for k in range(out_ref.shape[0]):
        blocks = [p[k] for p in parts]
        tops = [b[DIM + 1 : DIM + 2] for b in blocks]
        top = functools.reduce(jnp.maximum, tops)
        total = sum(b * jnp.exp2(t - top) for b, t in zip(blocks, tops))
        out_ref[slot_ref[k]] = jnp.where(row == DIM + 1, top, total)


def combine(slots, parts):
    vmem = pl.BlockSpec(memory_space=pltpu.VMEM)
    return pl.pallas_call(
        combine_kernel,
        out_shape=jax.ShapeDtypeStruct(parts[0].shape, f32),
        in_specs=[pl.BlockSpec(memory_space=pltpu.SMEM)] + [vmem] * len(parts),
        out_specs=vmem,
        compiler_params=pltpu.CompilerParams(vmem_limit_bytes=8 * 2**20),
        name="combine",
    )(slots, *parts)


def moments_kernel(got_ref, x_ref, label_ref, projected_ref, sums_ref):
    peers, _, cells = got_ref.shape
    top = got_ref[0, DIM : DIM + 8, :][1:2]
    for p in range(1, peers):
        top = jnp.maximum(top, got_ref[p, DIM : DIM + 8, :][1:2])
    total = jnp.zeros((72, cells), f32)
    for p in range(peers):
        block = got_ref[p]
        total = total + block * jnp.exp2(block[DIM + 1 : DIM + 2] - top)
    projected = total[:DIM] / total[DIM : DIM + 1]
    projected_ref[...] = projected
    moved = projected - x_ref[...].astype(f32)
    classes = lax.broadcasted_iota(jnp.int32, (FATES, cells), 0)
    indicator = jnp.where(classes == label_ref[...], 1.0, 0.0)
    across = (((1,), (1,)), ((), ()))
    by_class = lax.dot_general(
        moved, indicator, across, precision=lax.Precision.HIGHEST, preferred_element_type=f32
    )
    padded = jnp.concatenate([moved, jnp.zeros((128 - DIM, cells), f32)], 0)
    second = lax.dot_general(
        moved, padded, across, precision=lax.Precision.HIGHEST, preferred_element_type=f32
    )
    count = jnp.sum(indicator, 1, keepdims=True)
    lane = lax.broadcasted_iota(jnp.int32, (DIM, 128), 1)
    for q in range(FATES // DIM):
        second = jnp.where(lane == DIM + q, count[DIM * q : DIM * (q + 1)], second)
    sums_ref[:8] = by_class[:, :128].reshape(8, 8, 128)
    sums_ref[8:16] = by_class[:, 128:].reshape(8, 8, 128)
    sums_ref[16:24] = second.reshape(8, 8, 128)
    sums_ref[24:] = jnp.zeros((8, 8, 128), f32)


def moments(got, early, labels):
    return pl.pallas_call(
        moments_kernel,
        out_shape=(
            jax.ShapeDtypeStruct(early.shape, f32),
            jax.ShapeDtypeStruct((32, 8, 128), f32),
        ),
        in_specs=[pl.BlockSpec(memory_space=pltpu.VMEM)] * 3,
        out_specs=(pl.BlockSpec(memory_space=pltpu.VMEM),) * 2,
        compiler_params=pltpu.CompilerParams(vmem_limit_bytes=16 * 2**20),
        name="moments",
    )(got, early, labels)


def correlate_kernel(sums_ref, split_ref, out_ref, right, stage, sems, *, cells, block):
    genes = split_ref.shape[0]
    halves = [sums_ref[8 * h : 8 * h + 8].reshape(DIM, 128) for h in range(3)]
    by_class = jnp.concatenate(halves[:2], 1) / cells
    second = halves[2]
    flipped = second.T
    share = jnp.concatenate([flipped[DIM + q : DIM + q + 1] for q in range(FATES // DIM)], 1) / cells
    mean = jnp.sum(by_class, 1, keepdims=True)
    mean_row = jnp.broadcast_to(mean, (DIM, 128)).T[:1, :DIM]
    square = second[:, :DIM] / cells - mean * mean_row
    cross = (by_class - mean * share) / jnp.sqrt(share * (1.0 - share))
    both = jnp.concatenate([cross, square, square], 1)
    high = both.astype(bf16)
    low = (both - high.astype(f32)).astype(bf16)
    right[...] = jnp.concatenate([high, high, low, low], 0)

    def copy(k):
        rows = pl.ds(k * block, block)
        return pltpu.make_async_copy(stage.at[rows], out_ref.at[rows], sems.at[k])

    for k in range(genes // block):
        rows = split_ref[k * block : (k + 1) * block]
        product = jnp.dot(rows, right[...], preferred_element_type=f32)
        halves = rows[:, :128].astype(f32)
        variance = jnp.sum(product[:, FATES:] * halves, 1, keepdims=True) + EPSILON
        stage[k * block : (k + 1) * block] = product[:, :FATES] * (1.0 / jnp.sqrt(variance))
        copy(k).start()
    for k in range(genes // block):
        copy(k).wait()


def correlate(sums, split, cells, block=400):
    genes = split.shape[0]
    return pl.pallas_call(
        functools.partial(correlate_kernel, cells=cells, block=block),
        out_shape=jax.ShapeDtypeStruct((genes, FATES), f32),
        in_specs=[pl.BlockSpec(memory_space=pltpu.VMEM)] * 2,
        out_specs=pl.BlockSpec(memory_space=pl.ANY),
        scratch_shapes=[
            pltpu.VMEM((256, FATES + 128), bf16),
            pltpu.VMEM((genes, FATES), f32),
            pltpu.SemaphoreType.DMA((genes // block,)),
        ],
        compiler_params=pltpu.CompilerParams(vmem_limit_bytes=16 * 2**20),
        name="correlate",
    )(sums, split)


def shift(n, k):
    return [(i, (i + k) % n) for i in range(n)]


def shift_y(k):
    place = [y % 2 * 2 + y // 2 for y in range(4)]
    return [(place[y], place[(y + k) % 4]) for y in range(4)]


def exchange(blocks, axes):
    return lax.all_to_all(blocks, axes, 0, 0, tiled=False)


def spread(block, axes, size):
    return exchange(jnp.broadcast_to(block[None], (size,) + block.shape), axes)


def program(early, late, late_logs, labels, loadings):
    cells = float(early.shape[1] * math.prod(SIZES))
    turned = loadings.T
    high = lax.reduce_precision(turned, 8, 7)
    low = turned - high
    split = jnp.concatenate([high, low, high, low], 1).astype(bf16)

    swap = [(0, 1), (1, 0)]
    late_copies = pack(late, late_logs, SIZES[1])
    late_own = exchange(late_copies, "z")
    late_other = lax.ppermute(late_own, "core", swap)
    line = [early] + [lax.ppermute(early, "x", shift(4, k)) for k in range(1, 4)]
    line = jnp.stack(line)
    turns = [lax.ppermute(line, ("yl", "yh"), shift_y(k)) for k in range(1, 4)]
    back = jnp.arange(4, dtype=jnp.int32)
    slots = ((lax.axis_index("x") - back) % 4).astype(jnp.int32)
    own = ready(late_own)
    other = ready(late_other)
    lines = [line] + turns
    parts = {}
    for k in LINE_ORDER:
        parts[k] = attend_line(lines[k], own, other)
        if k:
            parts[k] = lax.ppermute(parts[k], ("yl", "yh"), shift_y(4 - k))
    got = exchange(combine(slots, [parts[k] for k in range(4)]), "x")
    projected, sums = moments(got, early, labels[None])
    sums = jnp.sum(exchange(sums, PLANE), 0)
    sums = jnp.sum(spread(sums, "z", SIZES[1]), 0)
    sums = spread(sums, PLANE, 32)
    return projected, correlate(sums, split, cells)


def solution(mesh):
    named = Mesh(mesh.devices.reshape(SIZES), AXES)
    in_specs = (P(None, AXES), P(None, AXES), P(AXES), P(AXES), P())
    out_specs = (P(None, AXES), P())
    return jax.shard_map(
        program, mesh=named, in_specs=in_specs, out_specs=out_specs, check_vma=False
    )
```

profile of v0, /device:TPU:1, one launch (start us, length us, event | category | flops | bytes accessed | tf_op | source)
XLA Modules:
  0.0 122.6 jit_solution(5996823807317815401)
XLA Ops:
  2.2 25.1 %all_to_all.25.late_ref = bf16[8,264,128]{2,1,0:T(8,128)(2,1)S(1)} all-to-all(bf16[8,264,128]{2,1,0:T(8,128)(2,1)S(1)} %pack.1), channel_id=1, replica_groups=mesh['yl'=2,'z'=8,'yh'=2,'x'=4,'core'=2] {'z'}, dimensions={0} | all-to-all | bytes 1081344 | tf_op jit(solution)/shard_map/all_to_all | solution.py:307
  27.4 2.5 %collective-permute-start.3 = (bf16[8,264,128]{2,1,0:T(8,128)(2,1)S(1)}, bf16[8,264,128]{2,1,0:T(8,128)(2,1)S(1)}, u32[]{:S(2)}, u32[]{:S(2)}) collective-permute-start(bf16[8,264,128]{2,1,0:T(8,128)(2,1)S(1)} %all_to_all.25.late_ref), channel_id=1, source_target_pairs={{0,1},{1,0},{2,3},{3,2},{4,5},{5,4},{6,7},{7,6},{8,9},{9,8},{10,11... | collective-permute-start | bytes 1622024 | tf_op jit(solution)/shard_map/ppermute | solution.py:324
  29.8 1.2 collective-permute-start
  31.0 2.5 %collective-permute-start.1 = (bf16[64,128]{1,0:T(8,128)(2,1)}, bf16[64,128]{1,0:T(8,128)(2,1)S(1)}, u32[]{:S(2)}, u32[]{:S(2)}) collective-permute-start(bf16[64,128]{1,0:T(8,128)(2,1)} %x_ref.1), channel_id=1, source_target_pairs={{0,4},{2,6},{4,0},{6,2},{1,5},{3,7},{5,1},{7,3},{8,12},{10,14},{12... | collective-permute-start | bytes 49160 | tf_op jit(solution)/shard_map/ppermute | solution.py:325
  33.5 1.2 collective-permute-start.2
  37.1 2.8 %collective-permute-start.8 = (bf16[4,64,128]{2,1,0:T(8,128)(2,1)S(1)}, bf16[4,64,128]{2,1,0:T(8,128)(2,1)S(1)}, u32[]{:S(2)}, u32[]{:S(2)}) collective-permute-start(bf16[4,64,128]{2,1,0:T(8,128)(2,1)S(1)} %pad_maximum_fusion.1.x_ref), channel_id=1, source_target_pairs={{0,136},{128,0},{8,128},{136,8},{1,137},{129,1},{9,129},{137,9},{2... | collective-permute-start | bytes 196616 | tf_op jit(solution)/shard_map/ppermute | solution.py:327
  42.5 5.6 %shard_map.73 = f32[4,72,128]{2,1,0:T(8,128)} custom-call(bf16[4,64,128]{2,1,0:T(8,128)(2,1)S(1)} %collective-permute-done.8.x_ref, bf16[4096,256]{1,0:T(8,128)(2,1)S(1)} %get-tuple-element.8.ya0, bf16[80,4096]{1,0:T(8,128)(2,1)S(1)} %get-tuple-element.9.yw0, bf16[4096,256]{1,0:T(8,128)(2,1)S(1)} %get-tuple-element.10.ya1, ...), custom_call_target="tpu_custom_call" | custom-call | tf_op jit(solution)/shard_map/pallas_call | solution.py:164
  48.1 1.6 %collective-permute-start.9 = (f32[4,72,128]{2,1,0:T(8,128)}, f32[4,72,128]{2,1,0:T(8,128)}, u32[]{:S(2)}, u32[]{:S(2)}) collective-permute-start(f32[4,72,128]{2,1,0:T(8,128)} %shard_map.73), channel_id=1, source_target_pairs={{0,128},{128,8},{8,136},{136,0},{1,129},{129,9},{9,137},{137,1},{2... | collective-permute-start | bytes 442376 | tf_op jit(solution)/shard_map/ppermute | solution.py:337
  49.7 5.6 %shard_map.72 = f32[4,72,128]{2,1,0:T(8,128)} custom-call(bf16[4,64,128]{2,1,0:T(8,128)(2,1)S(1)} %collective-permute-done.6.x_ref, bf16[4096,256]{1,0:T(8,128)(2,1)S(1)} %get-tuple-element.8.ya0, bf16[80,4096]{1,0:T(8,128)(2,1)S(1)} %get-tuple-element.9.yw0, bf16[4096,256]{1,0:T(8,128)(2,1)S(1)} %get-tuple-element.10.ya1, ...), custom_call_target="tpu_custom_call" | custom-call | tf_op jit(solution)/shard_map/pallas_call | solution.py:164
  55.3 1.5 %collective-permute-start.7 = (f32[4,72,128]{2,1,0:T(8,128)}, f32[4,72,128]{2,1,0:T(8,128)}, u32[]{:S(2)}, u32[]{:S(2)}) collective-permute-start(f32[4,72,128]{2,1,0:T(8,128)} %shard_map.72), channel_id=1, source_target_pairs={{0,8},{128,136},{8,0},{136,128},{1,9},{129,137},{9,1},{137,129},{2... | collective-permute-start | bytes 442376 | tf_op jit(solution)/shard_map/ppermute | solution.py:337
  56.8 5.6 %shard_map.71 = f32[4,72,128]{2,1,0:T(8,128)} custom-call(bf16[4,64,128]{2,1,0:T(8,128)(2,1)S(1)} %collective-permute-done.4.x_ref, bf16[4096,256]{1,0:T(8,128)(2,1)S(1)} %get-tuple-element.8.ya0, bf16[80,4096]{1,0:T(8,128)(2,1)S(1)} %get-tuple-element.9.yw0, bf16[4096,256]{1,0:T(8,128)(2,1)S(1)} %get-tuple-element.10.ya1, ...), custom_call_target="tpu_custom_call" | custom-call | tf_op jit(solution)/shard_map/pallas_call | solution.py:164
  63.3 1.6 %copy-done.1 = bf16[4096,256]{1,0:T(8,128)(2,1)S(1)} copy-done((bf16[4096,256]{1,0:T(8,128)(2,1)S(1)}, bf16[4096,256]{1,0:T(8,128)(2,1)}, u32[]{:S(2)}) %copy-start.1) | copy-done | bytes 2097176
  64.9 5.0 %shard_map.70.refs_0_ = f32[4,72,128]{2,1,0:T(8,128)S(1)} custom-call(bf16[4,64,128]{2,1,0:T(8,128)(2,1)S(1)} %pad_maximum_fusion.1.x_ref, bf16[4096,256]{1,0:T(8,128)(2,1)S(1)} %get-tuple-element.8.ya0, bf16[80,4096]{1,0:T(8,128)(2,1)S(1)} %get-tuple-element.9.yw0, bf16[4096,256]{1,0:T(8,128)(2,1)S(1)} %copy-done.1, bf16[80,4096]{1,0:T(8,128)(2,1)S(1)} %get-tuple-element.11.yw1), custom_call_target="tpu_custom_call" | custom-call | tf_op jit(solution)/shard_map/pallas_call | solution.py:164
  70.0 1.1 combine.1
  71.1 8.2 %all_to_all.26.got_ref = f32[4,72,128]{2,1,0:T(8,128)S(1)} all-to-all(f32[4,72,128]{2,1,0:T(8,128)S(1)} %combine.1), channel_id=1, replica_groups=mesh['yl'=2,'z'=8,'yh'=2,'x'=4,'core'=2] {'x'}, dimensions={0} | all-to-all | bytes 294912 | tf_op jit(solution)/shard_map/all_to_all | solution.py:307
  79.4 1.0 moments.1
  80.3 8.2 %all-to-all-start.2 = ((f32[32,8,128]{2,1,0:T(8,128)}), f32[32,8,128]{2,1,0:T(8,128)S(1)}, u32[]{:S(2)}, u32[]{:S(2)}) async-start(f32[32,8,128]{2,1,0:T(8,128)} %get-tuple-element.13), calls=%async_computation.2 | async-start | bytes 262144 | tf_op jit(solution)/shard_map/all_to_all | solution.py:307
  88.5 1.4 %copy.8 = f32[64,2000]{0,1:T(8,128)S(1)} copy(f32[64,2000]{1,0:T(8,128)} %param.9) | data formatting | bytes 1024000 | tf_op args[4]
  89.9 6.3 %all-to-all-done.2 = f32[32,8,128]{2,1,0:T(8,128)S(1)} async-done(((f32[32,8,128]{2,1,0:T(8,128)}), f32[32,8,128]{2,1,0:T(8,128)S(1)}, u32[]{:S(2)}, u32[]{:S(2)}) %all-to-all-start.2) | async-done | bytes 131104 | tf_op jit(solution)/shard_map/all_to_all | solution.py:307
  96.9 3.3 %all-to-all-start.3 = ((f32[8,8,128]{2,1,0:T(8,128)}), f32[8,8,128]{2,1,0:T(8,128)S(1)}, u32[]{:S(2)}, u32[]{:S(2)}) async-start(f32[8,8,128]{2,1,0:T(8,128)} %broadcast_in_dim.20), calls=%async_computation.3 | async-start | bytes 65536 | tf_op jit(solution)/shard_map/all_to_all | solution.py:307
  100.4 6.6 %all-to-all-done.3 = f32[8,8,128]{2,1,0:T(8,128)S(1)} async-done(((f32[8,8,128]{2,1,0:T(8,128)}), f32[8,8,128]{2,1,0:T(8,128)S(1)}, u32[]{:S(2)}, u32[]{:S(2)}) %all-to-all-start.3) | async-done | bytes 32800 | tf_op jit(solution)/shard_map/all_to_all | solution.py:307
  107.7 5.0 %all-to-all-start.4 = ((f32[32,8,128]{2,1,0:T(8,128)}), f32[32,8,128]{2,1,0:T(8,128)S(1)}, u32[]{:S(2)}, u32[]{:S(2)}) async-start(f32[32,8,128]{2,1,0:T(8,128)} %broadcast_in_dim.21), calls=%async_computation.4 | async-start | bytes 262144 | tf_op jit(solution)/shard_map/all_to_all | solution.py:307
  113.4 7.1 %all-to-all-done.4.sums_ref = f32[32,8,128]{2,1,0:T(8,128)S(1)} async-done(((f32[32,8,128]{2,1,0:T(8,128)}), f32[32,8,128]{2,1,0:T(8,128)S(1)}, u32[]{:S(2)}, u32[]{:S(2)}) %all-to-all-start.4) | async-done | bytes 131104 | tf_op jit(solution)/shard_map/all_to_all | solution.py:307
  120.4 2.0 %correlate.1 = f32[2000,256]{1,0:T(8,128)} custom-call(f32[32,8,128]{2,1,0:T(8,128)S(1)} %all-to-all-done.4.sums_ref, bf16[2000,256]{1,0:T(8,128)(2,1)S(1)} %pad_maximum_fusion.split_ref), custom_call_target="tpu_custom_call" | custom-call | tf_op jit(solution)/shard_map/correlate/pallas_call | solution.py:282
  (34 shorter events, 9.7 us)
Async XLA Ops:
  1.3 0.8 copy-start.2
  27.4 14.3 %collective-permute-start.3 = (bf16[8,264,128]{2,1,0:T(8,128)(2,1)S(1)}, bf16[8,264,128]{2,1,0:T(8,128)(2,1)S(1)}, u32[]{:S(2)}, u32[]{:S(2)}) collective-permute-start(bf16[8,264,128]{2,1,0:T(8,128)(2,1)S(1)} %all_to_all.25.late_ref), channel_id=1, source_target_pairs={{0,1},{1,0},{2,3},{3,2},{4,5},{5,4},{6,7},{7,6},{8,9},{9,8},{10,11... | collective-permute-start | bytes 1622024 | tf_op jit(solution)/shard_map/ppermute | solution.py:324
  29.8 4.8 %collective-permute-start = (bf16[64,128]{1,0:T(8,128)(2,1)}, bf16[64,128]{1,0:T(8,128)(2,1)S(1)}, u32[]{:S(2)}, u32[]{:S(2)}) collective-permute-start(bf16[64,128]{1,0:T(8,128)(2,1)} %x_ref.1), channel_id=1, source_target_pairs={{0,2},{2,4},{4,6},{6,0},{1,3},{3,5},{5,7},{7,1},{8,10},{10,12},{12... | collective-permute-start | bytes 49160 | tf_op jit(solution)/shard_map/ppermute | solution.py:325
  31.0 4.4 %collective-permute-start.1 = (bf16[64,128]{1,0:T(8,128)(2,1)}, bf16[64,128]{1,0:T(8,128)(2,1)S(1)}, u32[]{:S(2)}, u32[]{:S(2)}) collective-permute-start(bf16[64,128]{1,0:T(8,128)(2,1)} %x_ref.1), channel_id=1, source_target_pairs={{0,4},{2,6},{4,0},{6,2},{1,5},{3,7},{5,1},{7,3},{8,12},{10,14},{12... | collective-permute-start | bytes 49160 | tf_op jit(solution)/shard_map/ppermute | solution.py:325
  33.5 2.9 %collective-permute-start.2 = (bf16[64,128]{1,0:T(8,128)(2,1)}, bf16[64,128]{1,0:T(8,128)(2,1)S(1)}, u32[]{:S(2)}, u32[]{:S(2)}) collective-permute-start(bf16[64,128]{1,0:T(8,128)(2,1)} %x_ref.1), channel_id=1, source_target_pairs={{0,6},{2,0},{4,2},{6,4},{1,7},{3,1},{5,3},{7,5},{8,14},{10,8},{12,... | collective-permute-start | bytes 49160 | tf_op jit(solution)/shard_map/ppermute | solution.py:325
  37.1 5.4 %collective-permute-start.8 = (bf16[4,64,128]{2,1,0:T(8,128)(2,1)S(1)}, bf16[4,64,128]{2,1,0:T(8,128)(2,1)S(1)}, u32[]{:S(2)}, u32[]{:S(2)}) collective-permute-start(bf16[4,64,128]{2,1,0:T(8,128)(2,1)S(1)} %pad_maximum_fusion.1.x_ref), channel_id=1, source_target_pairs={{0,136},{128,0},{8,128},{136,8},{1,137},{129,1},{9,129},{137,9},{2... | collective-permute-start | bytes 196616 | tf_op jit(solution)/shard_map/ppermute | solution.py:327
  39.9 9.8 %collective-permute-start.6 = (bf16[4,64,128]{2,1,0:T(8,128)(2,1)S(1)}, bf16[4,64,128]{2,1,0:T(8,128)(2,1)S(1)}, u32[]{:S(2)}, u32[]{:S(2)}) collective-permute-start(bf16[4,64,128]{2,1,0:T(8,128)(2,1)S(1)} %pad_maximum_fusion.1.x_ref), channel_id=1, source_target_pairs={{0,8},{128,136},{8,0},{136,128},{1,9},{129,137},{9,1},{137,129},{2... | collective-permute-start | bytes 196616 | tf_op jit(solution)/shard_map/ppermute | solution.py:327
  40.3 16.6 %collective-permute-start.4 = (bf16[4,64,128]{2,1,0:T(8,128)(2,1)S(1)}, bf16[4,64,128]{2,1,0:T(8,128)(2,1)S(1)}, u32[]{:S(2)}, u32[]{:S(2)}) collective-permute-start(bf16[4,64,128]{2,1,0:T(8,128)(2,1)S(1)} %pad_maximum_fusion.1.x_ref), channel_id=1, source_target_pairs={{0,128},{128,8},{8,136},{136,0},{1,129},{129,9},{9,137},{137,1},{2... | collective-permute-start | bytes 196616 | tf_op jit(solution)/shard_map/ppermute | solution.py:327
  42.5 14.4 %copy-start = (bf16[4096,256]{1,0:T(8,128)(2,1)}, bf16[4096,256]{1,0:T(8,128)(2,1)S(1)}, u32[]{:S(2)}) copy-start(bf16[4096,256]{1,0:T(8,128)(2,1)S(1)} %get-tuple-element.10.ya1) | copy-start | bytes 6291460
  48.1 21.9 %collective-permute-start.9 = (f32[4,72,128]{2,1,0:T(8,128)}, f32[4,72,128]{2,1,0:T(8,128)}, u32[]{:S(2)}, u32[]{:S(2)}) collective-permute-start(f32[4,72,128]{2,1,0:T(8,128)} %shard_map.73), channel_id=1, source_target_pairs={{0,128},{128,8},{8,136},{136,0},{1,129},{129,9},{9,137},{137,1},{2... | collective-permute-start | bytes 442376 | tf_op jit(solution)/shard_map/ppermute | solution.py:337
  55.3 14.7 %collective-permute-start.7 = (f32[4,72,128]{2,1,0:T(8,128)}, f32[4,72,128]{2,1,0:T(8,128)}, u32[]{:S(2)}, u32[]{:S(2)}) collective-permute-start(f32[4,72,128]{2,1,0:T(8,128)} %shard_map.72), channel_id=1, source_target_pairs={{0,8},{128,136},{8,0},{136,128},{1,9},{129,137},{9,1},{137,129},{2... | collective-permute-start | bytes 442376 | tf_op jit(solution)/shard_map/ppermute | solution.py:337
  62.4 7.5 %collective-permute-start.5 = (f32[4,72,128]{2,1,0:T(8,128)}, f32[4,72,128]{2,1,0:T(8,128)}, u32[]{:S(2)}, u32[]{:S(2)}) collective-permute-start(f32[4,72,128]{2,1,0:T(8,128)} %shard_map.71), channel_id=1, source_target_pairs={{0,136},{128,0},{8,128},{136,8},{1,137},{129,1},{9,129},{137,9},{2... | collective-permute-start | bytes 442376 | tf_op jit(solution)/shard_map/ppermute | solution.py:337
  63.3 1.6 %copy-start.1 = (bf16[4096,256]{1,0:T(8,128)(2,1)S(1)}, bf16[4096,256]{1,0:T(8,128)(2,1)}, u32[]{:S(2)}) copy-start(bf16[4096,256]{1,0:T(8,128)(2,1)} %copy-done) | copy-start | bytes 6291460
  64.9 14.4 %copy-start.3 = (bf16[64,128]{1,0:T(8,128)(2,1)S(1)}, bf16[64,128]{1,0:T(8,128)(2,1)}, u32[]{:S(2)}) copy-start(bf16[64,128]{1,0:T(8,128)(2,1)} %x_ref.1) | copy-start | bytes 49156
  64.9 14.4 %copy-start.4 = (s32[128]{0:T(128)S(1)}, s32[128]{0:T(128)}, u32[]{:S(2)}) copy-start(s32[128]{0:T(128)} %param.8) | copy-start | bytes 1540
  80.3 15.9 %all-to-all-start.2 = ((f32[32,8,128]{2,1,0:T(8,128)}), f32[32,8,128]{2,1,0:T(8,128)S(1)}, u32[]{:S(2)}, u32[]{:S(2)}) async-start(f32[32,8,128]{2,1,0:T(8,128)} %get-tuple-element.13), calls=%async_computation.2 | async-start | bytes 262144 | tf_op jit(solution)/shard_map/all_to_all | solution.py:307
  96.9 10.1 %all-to-all-start.3 = ((f32[8,8,128]{2,1,0:T(8,128)}), f32[8,8,128]{2,1,0:T(8,128)S(1)}, u32[]{:S(2)}, u32[]{:S(2)}) async-start(f32[8,8,128]{2,1,0:T(8,128)} %broadcast_in_dim.20), calls=%async_computation.3 | async-start | bytes 65536 | tf_op jit(solution)/shard_map/all_to_all | solution.py:307
  107.7 12.8 %all-to-all-start.4 = ((f32[32,8,128]{2,1,0:T(8,128)}), f32[32,8,128]{2,1,0:T(8,128)S(1)}, u32[]{:S(2)}, u32[]{:S(2)}) async-start(f32[32,8,128]{2,1,0:T(8,128)} %broadcast_in_dim.21), calls=%async_computation.4 | async-start | bytes 262144 | tf_op jit(solution)/shard_map/all_to_all | solution.py:307
where the time goes:
time: 123 us
  blocking collectives  33.4 us (27%)
  starting transfers between devices  31.7 us (26%)
  Pallas kernels  27.4 us (22%)
  waiting for transfers between devices  21.7 us (18%)
  local copies, waits for them, and re-layouts  5.78 us (5%)
  other arithmetic  1.64 us (1%)
    all_to_all x2, blocking collectives, exchange(): return lax.all_to_all(blocks, axes, 0, 0, tiled=False)  33.4 us
    pallas_call x4, Pallas kernels, attend_line(): pl.pallas_call(functools.partial(line_kernel, tile=tile, sub=sub), out_sh...  21.8 us
    all_to_all x3, waiting for transfers between devices, exchange(): return lax.all_to_all(blocks, axes, 0, 0, tiled=False)  20 us
    all_to_all x3, starting transfers between devices, exchange(): return lax.all_to_all(blocks, axes, 0, 0, tiled=False)  16.5 us
    ppermute x3, starting transfers between devices, program(): lax.ppermute(early, 'x', shift(4, k))  4.81 us
    ppermute x3, starting transfers between devices, program(): parts[k] = lax.ppermute(parts[k], ('yl', 'yh'), shift_y(4 - k))  4.02 us
    ppermute x3, starting transfers between devices, program(): turns = [lax.ppermute(line, ('yl', 'yh'), shift_y(k)) for k in range(1, 4)]  3.85 us
    unnamed x11, local copies, waits for them, and re-layouts  3.81 us
  transfers between devices with their start and end apart: 13, of which 5 were waited for; matrix products, arithmetic and copies ran while one was open for 2% of the time, Pallas kernels for 19%

commit v1 on v0

--- a/solution.py
+++ b/solution.py
@@ -22,7 +22,7 @@
 
 AXES = ("yl", "z", "yh", "x", "core")
 SIZES = (2, 8, 2, 4, 2)
-PLANE = ("yl", "yh", "x", "core")
+PLANE = ("yl", "yh", "x")
 
 LINE_ORDER = (2, 1, 3, 0)
 
@@ -337,9 +337,10 @@
             parts[k] = lax.ppermute(parts[k], ("yl", "yh"), shift_y(4 - k))
     got = exchange(combine(slots, [parts[k] for k in range(4)]), "x")
     projected, sums = moments(got, early, labels[None])
-    sums = jnp.sum(exchange(sums, PLANE), 0)
+    sums = jnp.sum(exchange(sums.reshape(16, 16, 128), PLANE), 0)
+    sums = sums + lax.ppermute(sums, "core", swap)
     sums = jnp.sum(spread(sums, "z", SIZES[1]), 0)
-    sums = spread(sums, PLANE, 32)
+    sums = spread(sums, PLANE, 16).reshape(32, 8, 128)
     return projected, correlate(sums, split, cells)
 
 

time: 123 us -> 122 us (level)
  the two profiles are of different devices: /device:TPU:1 before, /device:TPU:2 now
where the time goes in v1:
time: 122 us
  blocking collectives  47.6 us (39%)
  Pallas kernels  27.1 us (22%)
  starting transfers between devices  22.2 us (18%)
  waiting for transfers between devices  16.6 us (14%)
  local copies, waits for them, and re-layouts  5.8 us (5%)
  other arithmetic  1.63 us (1%)
    all_to_all x3, blocking collectives, exchange(): return lax.all_to_all(blocks, axes, 0, 0, tiled=False)  47.6 us
    pallas_call x4, Pallas kernels, attend_line(): pl.pallas_call(functools.partial(line_kernel, tile=tile, sub=sub), out_sh...  21.8 us
    all_to_all x2, waiting for transfers between devices, exchange(): return lax.all_to_all(blocks, axes, 0, 0, tiled=False)  14.4 us
    all_to_all x2, starting transfers between devices, exchange(): return lax.all_to_all(blocks, axes, 0, 0, tiled=False)  8.11 us
    ppermute x3, starting transfers between devices, program(): lax.ppermute(early, 'x', shift(4, k))  4.76 us
    ppermute x3, starting transfers between devices, program(): turns = [lax.ppermute(line, ('yl', 'yh'), shift_y(k)) for k in range(1, 4)]  4.69 us
    ppermute x3, starting transfers between devices, program(): parts[k] = lax.ppermute(parts[k], ('yl', 'yh'), shift_y(4 - k))  4.55 us
    unnamed x11, local copies, waits for them, and re-layouts  3.81 us
  transfers between devices with their start and end apart: 13, of which 3 were waited for; matrix products, arithmetic and copies ran while one was open for 2% of the time, Pallas kernels for 19%

profile of v1, /device:TPU:2, one launch (start us, length us, event | category | flops | bytes accessed | tf_op | source)
XLA Modules:
  0.0 121.8 jit_solution(9845030885010072129)
XLA Ops:
  1.3 0.8 copy-done.2
  2.2 26.1 %all_to_all.25.late_ref = bf16[8,264,128]{2,1,0:T(8,128)(2,1)S(1)} all-to-all(bf16[8,264,128]{2,1,0:T(8,128)(2,1)S(1)} %pack.1), channel_id=1, replica_groups=mesh['yl'=2,'z'=8,'yh'=2,'x'=4,'core'=2] {'z'}, dimensions={0} | all-to-all | bytes 1081344 | tf_op jit(solution)/shard_map/all_to_all | solution.py:307
  28.3 1.5 %collective-permute-start = (bf16[64,128]{1,0:T(8,128)(2,1)}, bf16[64,128]{1,0:T(8,128)(2,1)S(1)}, u32[]{:S(2)}, u32[]{:S(2)}) collective-permute-start(bf16[64,128]{1,0:T(8,128)(2,1)} %x_ref.1), channel_id=1, source_target_pairs={{0,2},{2,4},{4,6},{6,0},{1,3},{3,5},{5,7},{7,1},{8,10},{10,12},{12... | collective-permute-start | bytes 49160 | tf_op jit(solution)/shard_map/ppermute | solution.py:325
  29.8 1.1 collective-permute-start.1
  30.9 2.2 %collective-permute-start.2 = (bf16[64,128]{1,0:T(8,128)(2,1)}, bf16[64,128]{1,0:T(8,128)(2,1)S(1)}, u32[]{:S(2)}, u32[]{:S(2)}) collective-permute-start(bf16[64,128]{1,0:T(8,128)(2,1)} %x_ref.1), channel_id=1, source_target_pairs={{0,6},{2,0},{4,2},{6,4},{1,7},{3,1},{5,3},{7,5},{8,14},{10,8},{12,... | collective-permute-start | bytes 49160 | tf_op jit(solution)/shard_map/ppermute | solution.py:325
  33.1 2.2 %collective-permute-done.1 = bf16[64,128]{1,0:T(8,128)(2,1)S(1)} collective-permute-done((bf16[64,128]{1,0:T(8,128)(2,1)}, bf16[64,128]{1,0:T(8,128)(2,1)S(1)}, u32[]{:S(2)}, u32[]{:S(2)}) %collective-permute-start.1) | collective-permute-done | bytes 16416 | tf_op jit(solution)/shard_map/ppermute | solution.py:325
  36.0 3.1 %collective-permute-start.8 = (bf16[4,64,128]{2,1,0:T(8,128)(2,1)S(1)}, bf16[4,64,128]{2,1,0:T(8,128)(2,1)S(1)}, u32[]{:S(2)}, u32[]{:S(2)}) collective-permute-start(bf16[4,64,128]{2,1,0:T(8,128)(2,1)S(1)} %pad_maximum_fusion.1.x_ref), channel_id=1, source_target_pairs={{0,136},{128,0},{8,128},{136,8},{1,137},{129,1},{9,129},{137,9},{2... | collective-permute-start | bytes 196616 | tf_op jit(solution)/shard_map/ppermute | solution.py:327
  39.7 1.0 collective-permute-start.4
  42.2 5.6 %shard_map.73 = f32[4,72,128]{2,1,0:T(8,128)} custom-call(bf16[4,64,128]{2,1,0:T(8,128)(2,1)S(1)} %collective-permute-done.8.x_ref, bf16[4096,256]{1,0:T(8,128)(2,1)S(1)} %get-tuple-element.8.ya0, bf16[80,4096]{1,0:T(8,128)(2,1)S(1)} %get-tuple-element.9.yw0, bf16[4096,256]{1,0:T(8,128)(2,1)S(1)} %get-tuple-element.10.ya1, ...), custom_call_target="tpu_custom_call" | custom-call | tf_op jit(solution)/shard_map/pallas_call | solution.py:164
  47.8 1.9 %collective-permute-start.9 = (f32[4,72,128]{2,1,0:T(8,128)}, f32[4,72,128]{2,1,0:T(8,128)}, u32[]{:S(2)}, u32[]{:S(2)}) collective-permute-start(f32[4,72,128]{2,1,0:T(8,128)} %shard_map.73), channel_id=1, source_target_pairs={{0,128},{128,8},{8,136},{136,0},{1,129},{129,9},{9,137},{137,1},{2... | collective-permute-start | bytes 442376 | tf_op jit(solution)/shard_map/ppermute | solution.py:337
  49.7 5.6 %shard_map.72 = f32[4,72,128]{2,1,0:T(8,128)} custom-call(bf16[4,64,128]{2,1,0:T(8,128)(2,1)S(1)} %collective-permute-done.6.x_ref, bf16[4096,256]{1,0:T(8,128)(2,1)S(1)} %get-tuple-element.8.ya0, bf16[80,4096]{1,0:T(8,128)(2,1)S(1)} %get-tuple-element.9.yw0, bf16[4096,256]{1,0:T(8,128)(2,1)S(1)} %get-tuple-element.10.ya1, ...), custom_call_target="tpu_custom_call" | custom-call | tf_op jit(solution)/shard_map/pallas_call | solution.py:164
  55.3 1.9 %collective-permute-start.7 = (f32[4,72,128]{2,1,0:T(8,128)}, f32[4,72,128]{2,1,0:T(8,128)}, u32[]{:S(2)}, u32[]{:S(2)}) collective-permute-start(f32[4,72,128]{2,1,0:T(8,128)} %shard_map.72), channel_id=1, source_target_pairs={{0,8},{128,136},{8,0},{136,128},{1,9},{129,137},{9,1},{137,129},{2... | collective-permute-start | bytes 442376 | tf_op jit(solution)/shard_map/ppermute | solution.py:337
  57.3 5.6 %shard_map.71 = f32[4,72,128]{2,1,0:T(8,128)} custom-call(bf16[4,64,128]{2,1,0:T(8,128)(2,1)S(1)} %collective-permute-done.4.x_ref, bf16[4096,256]{1,0:T(8,128)(2,1)S(1)} %get-tuple-element.8.ya0, bf16[80,4096]{1,0:T(8,128)(2,1)S(1)} %get-tuple-element.9.yw0, bf16[4096,256]{1,0:T(8,128)(2,1)S(1)} %get-tuple-element.10.ya1, ...), custom_call_target="tpu_custom_call" | custom-call | tf_op jit(solution)/shard_map/pallas_call | solution.py:164
  63.6 1.6 %copy-done.1 = bf16[4096,256]{1,0:T(8,128)(2,1)S(1)} copy-done((bf16[4096,256]{1,0:T(8,128)(2,1)S(1)}, bf16[4096,256]{1,0:T(8,128)(2,1)}, u32[]{:S(2)}) %copy-start.1) | copy-done | bytes 2097176
  65.2 5.0 %shard_map.70.refs_0_ = f32[4,72,128]{2,1,0:T(8,128)S(1)} custom-call(bf16[4,64,128]{2,1,0:T(8,128)(2,1)S(1)} %pad_maximum_fusion.1.x_ref, bf16[4096,256]{1,0:T(8,128)(2,1)S(1)} %get-tuple-element.8.ya0, bf16[80,4096]{1,0:T(8,128)(2,1)S(1)} %get-tuple-element.9.yw0, bf16[4096,256]{1,0:T(8,128)(2,1)S(1)} %copy-done.1, bf16[80,4096]{1,0:T(8,128)(2,1)S(1)} %get-tuple-element.11.yw1), custom_call_target="tpu_custom_call" | custom-call | tf_op jit(solution)/shard_map/pallas_call | solution.py:164
  70.3 1.1 combine.1
  71.4 10.1 %all_to_all.26.got_ref = f32[4,72,128]{2,1,0:T(8,128)S(1)} all-to-all(f32[4,72,128]{2,1,0:T(8,128)S(1)} %combine.1), channel_id=1, replica_groups=mesh['yl'=2,'z'=8,'yh'=2,'x'=4,'core'=2] {'x'}, dimensions={0} | all-to-all | bytes 294912 | tf_op jit(solution)/shard_map/all_to_all | solution.py:307
  82.2 11.4 %all_to_all.27 = f32[16,16,128]{2,1,0:T(8,128)S(1)} all-to-all(f32[16,16,128]{2,1,0:T(8,128)S(1)} %bitcast.11), channel_id=1, replica_groups=mesh['yl'=2,'z'=8,'yh'=2,'x'=4,'core'=2] {'yl','yh','x'}, dimensions={0} | all-to-all | bytes 262144 | tf_op jit(solution)/shard_map/all_to_all | solution.py:307
  93.7 1.4 %copy.8 = f32[64,2000]{0,1:T(8,128)S(1)} copy(f32[64,2000]{1,0:T(8,128)} %param.9) | data formatting | bytes 1024000 | tf_op args[4]
  95.7 3.4 %all-to-all-start.3 = ((f32[8,16,128]{2,1,0:T(8,128)}), f32[8,16,128]{2,1,0:T(8,128)S(1)}, u32[]{:S(2)}, u32[]{:S(2)}) async-start(f32[8,16,128]{2,1,0:T(8,128)} %broadcast_in_dim.20), calls=%async_computation.3 | async-start | bytes 131072 | tf_op jit(solution)/shard_map/all_to_all | solution.py:307
  99.2 8.3 %all-to-all-done.3 = f32[8,16,128]{2,1,0:T(8,128)S(1)} async-done(((f32[8,16,128]{2,1,0:T(8,128)}), f32[8,16,128]{2,1,0:T(8,128)S(1)}, u32[]{:S(2)}, u32[]{:S(2)}) %all-to-all-start.3) | async-done | bytes 65568 | tf_op jit(solution)/shard_map/all_to_all | solution.py:307
  108.3 4.8 %all-to-all-start.4 = ((f32[16,16,128]{2,1,0:T(8,128)}), f32[16,16,128]{2,1,0:T(8,128)S(1)}, u32[]{:S(2)}, u32[]{:S(2)}) async-start(f32[16,16,128]{2,1,0:T(8,128)} %broadcast_in_dim.21), calls=%async_computation.4 | async-start | bytes 262144 | tf_op jit(solution)/shard_map/all_to_all | solution.py:307
  113.7 6.0 %all-to-all-done.4 = f32[16,16,128]{2,1,0:T(8,128)S(1)} async-done(((f32[16,16,128]{2,1,0:T(8,128)}), f32[16,16,128]{2,1,0:T(8,128)S(1)}, u32[]{:S(2)}, u32[]{:S(2)}) %all-to-all-start.4) | async-done | bytes 131104 | tf_op jit(solution)/shard_map/all_to_all | solution.py:307
  119.7 2.0 %correlate.1 = f32[2000,256]{1,0:T(8,128)} custom-call(f32[32,8,128]{2,1,0:T(8,128)S(1)} %bitcast.10, bf16[2000,256]{1,0:T(8,128)(2,1)S(1)} %pad_maximum_fusion.split_ref), custom_call_target="tpu_custom_call" | custom-call | tf_op jit(solution)/shard_map/correlate/pallas_call | solution.py:282
  (36 shorter events, 7.3 us)
Async XLA Ops:
  1.3 0.8 copy-start.2
  28.3 13.1 %collective-permute-start.3 = (bf16[8,264,128]{2,1,0:T(8,128)(2,1)S(1)}, bf16[8,264,128]{2,1,0:T(8,128)(2,1)S(1)}, u32[]{:S(2)}, u32[]{:S(2)}) collective-permute-start(bf16[8,264,128]{2,1,0:T(8,128)(2,1)S(1)} %all_to_all.25.late_ref), channel_id=1, source_target_pairs={{0,1},{1,0},{2,3},{3,2},{4,5},{5,4},{6,7},{7,6},{8,9},{9,8},{10,11... | collective-permute-start | bytes 1622024 | tf_op jit(solution)/shard_map/ppermute | solution.py:324
  28.3 4.8 %collective-permute-start = (bf16[64,128]{1,0:T(8,128)(2,1)}, bf16[64,128]{1,0:T(8,128)(2,1)S(1)}, u32[]{:S(2)}, u32[]{:S(2)}) collective-permute-start(bf16[64,128]{1,0:T(8,128)(2,1)} %x_ref.1), channel_id=1, source_target_pairs={{0,2},{2,4},{4,6},{6,0},{1,3},{3,5},{5,7},{7,1},{8,10},{10,12},{12... | collective-permute-start | bytes 49160 | tf_op jit(solution)/shard_map/ppermute | solution.py:325
  29.8 5.5 %collective-permute-start.1 = (bf16[64,128]{1,0:T(8,128)(2,1)}, bf16[64,128]{1,0:T(8,128)(2,1)S(1)}, u32[]{:S(2)}, u32[]{:S(2)}) collective-permute-start(bf16[64,128]{1,0:T(8,128)(2,1)} %x_ref.1), channel_id=1, source_target_pairs={{0,4},{2,6},{4,0},{6,2},{1,5},{3,7},{5,1},{7,3},{8,12},{10,14},{12... | collective-permute-start | bytes 49160 | tf_op jit(solution)/shard_map/ppermute | solution.py:325
  30.9 4.3 %collective-permute-start.2 = (bf16[64,128]{1,0:T(8,128)(2,1)}, bf16[64,128]{1,0:T(8,128)(2,1)S(1)}, u32[]{:S(2)}, u32[]{:S(2)}) collective-permute-start(bf16[64,128]{1,0:T(8,128)(2,1)} %x_ref.1), channel_id=1, source_target_pairs={{0,6},{2,0},{4,2},{6,4},{1,7},{3,1},{5,3},{7,5},{8,14},{10,8},{12,... | collective-permute-start | bytes 49160 | tf_op jit(solution)/shard_map/ppermute | solution.py:325
  36.0 6.2 %collective-permute-start.8 = (bf16[4,64,128]{2,1,0:T(8,128)(2,1)S(1)}, bf16[4,64,128]{2,1,0:T(8,128)(2,1)S(1)}, u32[]{:S(2)}, u32[]{:S(2)}) collective-permute-start(bf16[4,64,128]{2,1,0:T(8,128)(2,1)S(1)} %pad_maximum_fusion.1.x_ref), channel_id=1, source_target_pairs={{0,136},{128,0},{8,128},{136,8},{1,137},{129,1},{9,129},{137,9},{2... | collective-permute-start | bytes 196616 | tf_op jit(solution)/shard_map/ppermute | solution.py:327
  39.1 10.6 %collective-permute-start.6 = (bf16[4,64,128]{2,1,0:T(8,128)(2,1)S(1)}, bf16[4,64,128]{2,1,0:T(8,128)(2,1)S(1)}, u32[]{:S(2)}, u32[]{:S(2)}) collective-permute-start(bf16[4,64,128]{2,1,0:T(8,128)(2,1)S(1)} %pad_maximum_fusion.1.x_ref), channel_id=1, source_target_pairs={{0,8},{128,136},{8,0},{136,128},{1,9},{129,137},{9,1},{137,129},{2... | collective-permute-start | bytes 196616 | tf_op jit(solution)/shard_map/ppermute | solution.py:327
  39.7 17.5 %collective-permute-start.4 = (bf16[4,64,128]{2,1,0:T(8,128)(2,1)S(1)}, bf16[4,64,128]{2,1,0:T(8,128)(2,1)S(1)}, u32[]{:S(2)}, u32[]{:S(2)}) collective-permute-start(bf16[4,64,128]{2,1,0:T(8,128)(2,1)S(1)} %pad_maximum_fusion.1.x_ref), channel_id=1, source_target_pairs={{0,128},{128,8},{8,136},{136,0},{1,129},{129,9},{9,137},{137,1},{2... | collective-permute-start | bytes 196616 | tf_op jit(solution)/shard_map/ppermute | solution.py:327
  42.2 15.1 %copy-start = (bf16[4096,256]{1,0:T(8,128)(2,1)}, bf16[4096,256]{1,0:T(8,128)(2,1)S(1)}, u32[]{:S(2)}) copy-start(bf16[4096,256]{1,0:T(8,128)(2,1)S(1)} %get-tuple-element.10.ya1) | copy-start | bytes 6291460
  47.8 22.4 %collective-permute-start.9 = (f32[4,72,128]{2,1,0:T(8,128)}, f32[4,72,128]{2,1,0:T(8,128)}, u32[]{:S(2)}, u32[]{:S(2)}) collective-permute-start(f32[4,72,128]{2,1,0:T(8,128)} %shard_map.73), channel_id=1, source_target_pairs={{0,128},{128,8},{8,136},{136,0},{1,129},{129,9},{9,137},{137,1},{2... | collective-permute-start | bytes 442376 | tf_op jit(solution)/shard_map/ppermute | solution.py:337
  55.3 14.9 %collective-permute-start.7 = (f32[4,72,128]{2,1,0:T(8,128)}, f32[4,72,128]{2,1,0:T(8,128)}, u32[]{:S(2)}, u32[]{:S(2)}) collective-permute-start(f32[4,72,128]{2,1,0:T(8,128)} %shard_map.72), channel_id=1, source_target_pairs={{0,8},{128,136},{8,0},{136,128},{1,9},{129,137},{9,1},{137,129},{2... | collective-permute-start | bytes 442376 | tf_op jit(solution)/shard_map/ppermute | solution.py:337
  62.9 7.4 %collective-permute-start.5 = (f32[4,72,128]{2,1,0:T(8,128)}, f32[4,72,128]{2,1,0:T(8,128)}, u32[]{:S(2)}, u32[]{:S(2)}) collective-permute-start(f32[4,72,128]{2,1,0:T(8,128)} %shard_map.71), channel_id=1, source_target_pairs={{0,136},{128,0},{8,128},{136,8},{1,137},{129,1},{9,129},{137,9},{2... | collective-permute-start | bytes 442376 | tf_op jit(solution)/shard_map/ppermute | solution.py:337
  63.6 1.6 %copy-start.1 = (bf16[4096,256]{1,0:T(8,128)(2,1)S(1)}, bf16[4096,256]{1,0:T(8,128)(2,1)}, u32[]{:S(2)}) copy-start(bf16[4096,256]{1,0:T(8,128)(2,1)} %copy-done) | copy-start | bytes 6291460
  65.2 16.3 %copy-start.3 = (bf16[64,128]{1,0:T(8,128)(2,1)S(1)}, bf16[64,128]{1,0:T(8,128)(2,1)}, u32[]{:S(2)}) copy-start(bf16[64,128]{1,0:T(8,128)(2,1)} %x_ref.1) | copy-start | bytes 49156
  65.2 16.3 %copy-start.4 = (s32[128]{0:T(128)S(1)}, s32[128]{0:T(128)}, u32[]{:S(2)}) copy-start(s32[128]{0:T(128)} %param.8) | copy-start | bytes 1540
  93.6 1.5 %collective-permute-start.10 = (f32[16,128]{1,0:T(8,128)S(1)}, f32[16,128]{1,0:T(8,128)S(1)}, u32[]{:S(2)}, u32[]{:S(2)}) collective-permute-start(f32[16,128]{1,0:T(8,128)S(1)} %reduce_sum.18), channel_id=1, source_target_pairs={{0,1},{1,0},{2,3},{3,2},{4,5},{5,4},{6,7},{7,6},{8,9},{9,8},{10,11... | collective-permute-start | bytes 24584 | tf_op jit(solution)/shard_map/ppermute | solution.py:341
  95.7 11.9 %all-to-all-start.3 = ((f32[8,16,128]{2,1,0:T(8,128)}), f32[8,16,128]{2,1,0:T(8,128)S(1)}, u32[]{:S(2)}, u32[]{:S(2)}) async-start(f32[8,16,128]{2,1,0:T(8,128)} %broadcast_in_dim.20), calls=%async_computation.3 | async-start | bytes 131072 | tf_op jit(solution)/shard_map/all_to_all | solution.py:307
  108.3 11.5 %all-to-all-start.4 = ((f32[16,16,128]{2,1,0:T(8,128)}), f32[16,16,128]{2,1,0:T(8,128)S(1)}, u32[]{:S(2)}, u32[]{:S(2)}) async-start(f32[16,16,128]{2,1,0:T(8,128)} %broadcast_in_dim.21), calls=%async_computation.4 | async-start | bytes 262144 | tf_op jit(solution)/shard_map/all_to_all | solution.py:307
